TPU v7x, 32 devices: a whole 2x2x4 slice. The times are simulated.
32 devices in a mesh: chan: 4 (over y, core), tm: 8 (over z, x).
Axes of the slice: x: 2, y: 2, z: 4, core: 2. Of those that a mesh axis runs over, the one named last changes fastest.
Arguments:
- readings: float32 [8192, 8192], P('chan', 'tm'), may hold values from -8 to 8
- channel_start: float32 [8192, 64], P(('chan', 'tm')), may hold values from -6 to 6
- time_start: float32 [8192, 64], P(('tm', 'chan')), may hold values from -0.75 to 0.75
Outputs:
- outliers: float32 [8192, 8192], P('chan', 'tm')
- channel_factors: float32 [8192, 64], P(('chan', 'tm'))
- time_factors: float32 [8192, 64], P(('tm', 'chan'))
All inputs are finite; a program needn't handle non-finite values.
Results may differ from a plain program's by a relative error of at most 0.00019.
Values sent between devices are 32-bit elements; how exact they have to be, the bound alone decides.
A program may use at most 128 MiB of HBM per device.

v0:
```python
import jax
import jax.numpy as jnp
from jax import lax
from jax.sharding import PartitionSpec as P

ITERS = 2


threshold_level = 1.5
ridge_weight = 8.0


def rows_product(first, second):
    return lax.dot_general(
        first,
        second,
        (((1,), (1,)), ((), ())),
        precision=lax.Precision.HIGHEST,
        preferred_element_type=jnp.float32,
    )


def cols_product(first, second):
    return lax.dot_general(
        first,
        second,
        (((0,), (0,)), ((), ())),
        precision=lax.Precision.HIGHEST,
        preferred_element_type=jnp.float32,
    )


def solve_ridge(partial_value, gram):
    factor_chol = jnp.linalg.cholesky(gram)
    middle = lax.linalg.triangular_solve(
        factor_chol, partial_value, left_side=False, lower=True, transpose_a=True
    )
    return lax.linalg.triangular_solve(
        factor_chol, middle, left_side=False, lower=True, transpose_a=False
    )


def gram_sum(piece, identity):
    local_gram = cols_product(piece, piece)
    return lax.psum(local_gram, ("chan", "tm")) + ridge_weight * identity


def gather_left(piece):
    return lax.all_gather(piece, "tm", axis=0, tiled=True)


def gather_right(piece):
    return lax.all_gather(piece, "chan", axis=0, tiled=True)


def shards(readings, channel_start, time_start):
    factor_width = channel_start.shape[1]
    identity = jnp.eye(factor_width, dtype=jnp.float32)
    left_count = channel_start.shape[0]
    right_count = time_start.shape[0]
    left_piece = channel_start
    right_piece = time_start
    left_block = gather_left(left_piece)
    right_block = gather_right(right_piece)
    outliers = readings
    for sweep in range(ITERS):
        residue = readings - rows_product(left_block, right_block)
        outliers = residue - jnp.clip(residue, -threshold_level, threshold_level)
        cleaned = readings - outliers
        gram_right = gram_sum(right_piece, identity)
        left_total = lax.psum(
            jnp.dot(
                cleaned,
                right_block,
                precision=lax.Precision.HIGHEST,
                preferred_element_type=jnp.float32,
            ),
            "tm",
        )
        left_block = solve_ridge(left_total, gram_right)
        left_piece = lax.dynamic_slice_in_dim(
            left_block, lax.axis_index("tm") * left_count, left_count, 0
        )
        gram_left = gram_sum(left_piece, identity)
        right_total = lax.psum(cols_product(cleaned, left_block), "chan")
        right_block = solve_ridge(right_total, gram_left)
        right_piece = lax.dynamic_slice_in_dim(
            right_block, lax.axis_index("chan") * right_count, right_count, 0
        )
    return (outliers, left_piece, right_piece)


def solution(mesh):
    in_specs = (P("chan", "tm"), P(("chan", "tm"), None), P(("tm", "chan"), None))
    out_specs = (P("chan", "tm"), P(("chan", "tm"), None), P(("tm", "chan"), None))
    return jax.shard_map(shards, mesh=mesh, in_specs=in_specs, out_specs=out_specs, check_vma=False)
```

profile of v0, /device:TPU:0, one launch (start us, length us, event | category | flops | bytes accessed | tf_op | source)
XLA Modules:
  0.0 445.1 jit_solution(6114165455940073401)
XLA Ops:
  7.2 7.5 %all_gather.7 = f32[1024,64]{0,1:T(8,128)S(1)} all-gather(f32[256,64]{0,1:T(8,128)} %param.14), channel_id=1, replica_groups=mesh['chan'=4,'tm'=8] {'chan'}, dimensions={0}, use_global_device_ids=true | all-gather | bytes 327680 | tf_op jit(solution)/shard_map/all_gather | solution.py:53
  14.7 32.1 %all_gather.6 = f32[2048,64]{0,1:T(8,128)S(1)} all-gather(f32[256,64]{0,1:T(8,128)} %param.13), channel_id=1, replica_groups=mesh['chan'=4,'tm'=8] {'tm'}, dimensions={0}, use_global_device_ids=true | all-gather | bytes 589824 | tf_op jit(solution)/shard_map/all_gather | solution.py:49
  46.7 9.9 %fusion = f32[2048,1024]{1,0:T(8,128)S(1)} fusion(f32[2048,1024]{1,0:T(8,128)} %param.12, f32[2048,64]{0,1:T(8,128)S(1)} %all_gather.6, f32[1024,64]{0,1:T(8,128)S(1)} %all_gather.7), kind=kOutput, calls=%fused_computation.2 | convolution fusion | flops 1619001344 | bytes 17563648 | tf_op jit(solution)/shard_map/dot_general | solution.py:14
  56.6 3.4 copy-done
  60.0 7.8 %fusion.25 = f32[2048,64]{1,0:T(8,128)} fusion(f32[2048,1024]{1,0:T(8,128)S(1)} %fusion, f32[1024,64]{0,1:T(8,128)S(1)} %all_gather.7), kind=kOutput, calls=%fused_computation.60 | convolution fusion | flops 1610612736 | bytes 9175040 | tf_op jit(solution)/shard_map/dot_general | solution.py:72
  67.9 0.2 fusion.24
  68.1 40.1 %psum.56 = f32[64,64]{0,1:T(8,128)S(1)} all-reduce(f32[64,64]{0,1:T(8,128)S(1)} %fusion.24), channel_id=1, replica_groups=mesh['chan'=4,'tm'=8] {'chan','tm'}, use_global_device_ids=true, to_apply=%region_0.1 | all-reduce | flops 4096 | bytes 32768 | tf_op jit(solution)/shard_map/psum | solution.py:45
  108.2 0.1 copy.7
  108.4 5.8 %cholesky.74 = f32[64,64]{1,0:T(8,128)S(1)} custom-call(f32[64,64]{1,0:T(8,128)S(1)} %fusion.20), custom_call_target="Cholesky" | custom-call | tf_op jit(solution)/shard_map/jit(cholesky)/cholesky | solution.py:34
  114.2 0.6 compare_reduce_fusion.3
  114.9 0.7 fusion.5
  115.5 4.9 %custom-call.19 = f32[1,64,64]{1,2,0:T(8,128)S(1)} custom-call(f32[1,64,64]{2,1,0:T(8,128)S(1)} %fusion.5), custom_call_target="InvertDiagBlocksLowerTriangular" | custom-call | tf_op jit(solution)/shard_map/triangular_solve/custom-call.2 | solution.py:38
  120.4 27.0 %all-reduce.5.cloned.1.call-done = f32[2048,64]{1,0:T(8,128)} async-done(((f32[2048,64]{1,0:T(8,128)}), f32[2048,64]{1,0:T(8,128)}) %all-reduce.5.cloned.1.call-update) | async-done | bytes 524304 | tf_op jit(solution)/shard_map/psum | solution.py:71
  147.5 2.5 convolution_bitcast_fusion.3
  150.0 0.6 convolution_bitcast_fusion.1
  150.6 16.2 %fusion.26 = f32[1024,64]{1,0:T(8,128)} fusion(f32[2048,1024]{1,0:T(8,128)} %copy-done, f32[2048,64]{0,1:T(8,128)S(1)} %convolution_bitcast_fusion.1), kind=kOutput, calls=%fused_computation.61 | convolution fusion | flops 1610612736 | bytes 9175040 | tf_op jit(solution)/shard_map/dot_general | solution.py:24
  166.9 0.2 fusion.3
  167.1 40.0 %psum.58 = f32[64,64]{0,1:T(8,128)S(1)} all-reduce(f32[64,64]{0,1:T(8,128)S(1)} %fusion.3), channel_id=1, replica_groups=mesh['chan'=4,'tm'=8] {'chan','tm'}, use_global_device_ids=true, to_apply=%region_4.8 | all-reduce | flops 4096 | bytes 32768 | tf_op jit(solution)/shard_map/psum | solution.py:45
  207.1 0.1 copy.9
  207.2 5.8 %cholesky.85 = f32[64,64]{1,0:T(8,128)S(1)} custom-call(f32[64,64]{1,0:T(8,128)S(1)} %fusion.17), custom_call_target="Cholesky" | custom-call | tf_op jit(solution)/shard_map/jit(cholesky)/cholesky | solution.py:34
  213.0 0.6 compare_reduce_fusion.2
  213.7 0.7 fusion.6
  214.3 4.9 %custom-call.21 = f32[1,64,64]{1,2,0:T(8,128)S(1)} custom-call(f32[1,64,64]{2,1,0:T(8,128)S(1)} %fusion.6), custom_call_target="InvertDiagBlocksLowerTriangular" | custom-call | tf_op jit(solution)/shard_map/triangular_solve/custom-call.4 | solution.py:38
  219.3 1.7 convolution_bitcast_fusion.5
  221.0 0.4 convolution_bitcast_fusion.7
  221.4 13.3 %fusion.23 = (f32[2048,1024]{1,0:T(8,128)}, f32[2048,1024]{1,0:T(8,128)}) fusion(f32[2048,1024]{1,0:T(8,128)} %param.12, f32[2048,64]{0,1:T(8,128)S(1)} %convolution_bitcast_fusion.1, f32[1024,64]{0,1:T(8,128)S(1)} %convolution_bitcast_fusion.7), kind=kOutput, calls=%fused_computation.58 | convolution fusion | flops 1619001344 | bytes 25952256 | tf_op jit(solution)/shard_map/dot_general | solution.py:14
  234.7 0.2 fusion.1
  234.9 39.7 %psum.60 = f32[64,64]{0,1:T(8,128)S(1)} all-reduce(f32[64,64]{0,1:T(8,128)S(1)} %fusion.1), channel_id=1, replica_groups=mesh['chan'=4,'tm'=8] {'chan','tm'}, use_global_device_ids=true, to_apply=%region_6.12 | all-reduce | flops 4096 | bytes 32768 | tf_op jit(solution)/shard_map/psum | solution.py:45
  274.6 0.1 copy.11
  274.7 9.8 %fusion.27 = f32[2048,64]{1,0:T(8,128)} fusion(f32[2048,1024]{1,0:T(8,128)} %get-tuple-element.6, f32[1024,64]{0,1:T(8,128)S(1)} %convolution_bitcast_fusion.7), kind=kOutput, calls=%fused_computation.62 | convolution fusion | flops 1610612736 | bytes 9175040 | tf_op jit(solution)/shard_map/dot_general | solution.py:72
  284.5 0.3 all-reduce.11.cloned.1.call-start
  284.8 5.8 %cholesky.96 = f32[64,64]{1,0:T(8,128)S(1)} custom-call(f32[64,64]{1,0:T(8,128)S(1)} %fusion.14), custom_call_target="Cholesky" | custom-call | tf_op jit(solution)/shard_map/jit(cholesky)/cholesky | solution.py:34
  290.7 0.6 compare_reduce_fusion.1
  291.3 0.7 fusion.7
  292.0 4.9 %custom-call.23 = f32[1,64,64]{1,2,0:T(8,128)S(1)} custom-call(f32[1,64,64]{2,1,0:T(8,128)S(1)} %fusion.7), custom_call_target="InvertDiagBlocksLowerTriangular" | custom-call | tf_op jit(solution)/shard_map/triangular_solve/custom-call.2 | solution.py:38
  296.9 66.5 %all-reduce.9.cloned.1.call-done = f32[2048,64]{1,0:T(8,128)} async-done(((f32[2048,64]{1,0:T(8,128)}), f32[2048,64]{1,0:T(8,128)}) %all-reduce.9.cloned.1.call-update) | async-done | bytes 524304 | tf_op jit(solution)/shard_map/psum | solution.py:71
  363.4 2.5 convolution_bitcast_fusion.2
  365.9 0.6 convolution_bitcast_fusion
  366.5 16.2 %fusion.29 = f32[1024,64]{1,0:T(8,128)} fusion(f32[2048,1024]{1,0:T(8,128)} %get-tuple-element.6, f32[2048,64]{0,1:T(8,128)S(1)} %convolution_bitcast_fusion), kind=kOutput, calls=%fused_computation.64 | convolution fusion | flops 1610612736 | bytes 9175040 | tf_op jit(solution)/shard_map/dot_general | solution.py:24
  382.8 0.2 fusion.28
  383.0 40.0 %psum.62 = f32[64,64]{0,1:T(8,128)S(1)} all-reduce(f32[64,64]{0,1:T(8,128)S(1)} %fusion.28), channel_id=1, replica_groups=mesh['chan'=4,'tm'=8] {'chan','tm'}, use_global_device_ids=true, to_apply=%region_8.14 | all-reduce | flops 4096 | bytes 32768 | tf_op jit(solution)/shard_map/psum | solution.py:45
  423.1 5.8 %cholesky.107 = f32[64,64]{1,0:T(8,128)S(1)} custom-call(f32[64,64]{1,0:T(8,128)S(1)} %fusion.11), custom_call_target="Cholesky" | custom-call | tf_op jit(solution)/shard_map/jit(cholesky)/cholesky | solution.py:34
  429.0 0.6 compare_reduce_fusion
  429.7 0.7 fusion.8
  430.3 4.9 %custom-call.25 = f32[1,64,64]{1,2,0:T(8,128)S(1)} custom-call(f32[1,64,64]{2,1,0:T(8,128)S(1)} %fusion.8), custom_call_target="InvertDiagBlocksLowerTriangular" | custom-call | tf_op jit(solution)/shard_map/triangular_solve/custom-call.4 | solution.py:38
  435.3 1.7 convolution_bitcast_fusion.4
  437.0 0.4 convolution_bitcast_fusion.6
  437.4 0.6 constant_dynamic-slice_fusion
  (28 shorter events, 0.6 us)
Async XLA Ops:
  7.2 140.3 %all-reduce.5.cloned.1.call-start = ((), (), s32[]{:S(2)}) async-start(), calls=%async_computation | async-start | bytes 2097152 | tf_op jit(solution)/shard_map/psum | solution.py:71
  56.6 3.4 copy-start
  60.0 7.9 %copy-start.1 = (f32[256,64]{0,1:T(8,128)S(1)}, f32[256,64]{0,1:T(8,128)}, u32[]{:S(2)}) copy-start(f32[256,64]{0,1:T(8,128)} %param.14) | copy-start | bytes 196612
  67.8 151.5 %all-reduce.7.cloned.1.call-start = ((), (), s32[]{:S(2)}) async-start(), calls=%async_computation.1 | async-start | bytes 1048576 | tf_op jit(solution)/shard_map/psum | solution.py:85
  166.8 196.6 %all-reduce.9.cloned.1.call-start = ((), (), s32[]{:S(2)}) async-start(), calls=%async_computation.2 | async-start | bytes 2097152 | tf_op jit(solution)/shard_map/psum | solution.py:71
  284.5 150.8 %all-reduce.11.cloned.1.call-start = ((), (), s32[]{:S(2)}) async-start(), calls=%async_computation.3 | async-start | bytes 1048576 | tf_op jit(solution)/shard_map/psum | solution.py:85
  382.7 55.3 %copy-start.2 = (f32[256,64]{0,1:T(8,128)}, f32[256,64]{0,1:T(8,128)S(1)}, u32[]{:S(2)}) copy-start(f32[256,64]{0,1:T(8,128)S(1)} %constant_dynamic-slice_fusion.1) | copy-start | bytes 196612
Sparse Core Ops, SparseCore 0:
  67.9 79.4 all-reduce.4
  166.9 33.1 all-reduce.6
  284.6 78.7 all-reduce.8
  382.9 33.1 all-reduce.10
where the time goes:
time: 454 us; the launch traced here: 445 us
  blocking collectives  199 us (44%)
  waiting for transfers between devices  93.7 us (21%)
  matrix products  84.4 us (19%)
  other arithmetic  48.4 us (11%)
  between operations  14.6 us (3%)
    psum x4, blocking collectives, gram_sum(): return lax.psum(local_gram, ('chan', 'tm')) + ridge_weight * identity  160 us
    psum x2, waiting for transfers between devices, shards(): lax.psum(jnp.dot(cleaned, right_block, precision=lax.Precision.HIGHEST, p...  93.6 us
    dot_general x6, matrix products, cols_product(): lax.dot_general(first, second, (((0,), (0,)), ((), ())), precision=lax.Pr...  33.3 us
    all_gather x1, blocking collectives, gather_left(): return lax.all_gather(piece, 'tm', axis=0, tiled=True)  32.1 us
    another operation x12, other arithmetic, solve_ridge(): factor_chol = jnp.linalg.cholesky(gram)  26.1 us
    dot_general x2, matrix products, rows_product(): lax.dot_general(first, second, (((1,), (1,)), ((), ())), precision=lax.Pr...  23.2 us
    another operation x8, other arithmetic, solve_ridge(): lax.linalg.triangular_solve(factor_chol, middle, left_side=False, lower=T...  22.2 us
    dot_general x2, matrix products, shards(): jnp.dot(cleaned, right_block, precision=lax.Precision.HIGHEST, preferred_...  17.6 us
  transfers between devices with their start and end apart: 4, of which 2 were waited for; matrix products, arithmetic and copies ran while one was open for 11% of the time, Pallas kernels for 0%

commit v1 on v0

v1 whole, which is shorter than its diff:
```python
import functools

import jax
import jax.numpy as jnp
from jax import lax
from jax.experimental import pallas as pl
from jax.experimental.pallas import tpu as pltpu
from jax.sharding import PartitionSpec as P

ITERS = 2
LEVEL = 1.5
RIDGE = 8.0
MESH = pl.DeviceIdType.MESH
HIGHEST = lax.Precision.HIGHEST


def split(value):
    high = value.astype(jnp.bfloat16)
    low = (value - high.astype(jnp.float32)).astype(jnp.bfloat16)
    return high, low


def stacked(value):
    high = value.astype(jnp.bfloat16).astype(jnp.float32)
    return jnp.concatenate([high, value - high], axis=0)


def dot(first, second):
    return jnp.dot(first, second, preferred_element_type=jnp.float32)


def outer_gram(value):
    return lax.dot_general(value, value, (((1,), (1,)), ((), ())), precision=HIGHEST,
                           preferred_element_type=jnp.float32)


def inverse(gram):
    rank = gram.shape[0]
    rows = lax.broadcasted_iota(jnp.int32, (rank, rank), 0)
    cols = lax.broadcasted_iota(jnp.int32, (rank, rank), 1)
    for k in range(rank):
        row = gram[k:k + 1, :]
        col = gram[:, k:k + 1]
        inv = 1.0 / gram[k:k + 1, k:k + 1]
        scaled = jnp.where(cols[:1] == k, 1.0, row) * inv
        rest = jnp.where(cols == k, 0.0, gram) - col * scaled
        gram = jnp.where(rows == k, scaled, rest)
    return gram


def kernel(n, m, x_hbm, l0, r0, out_hbm, lout, rout,
           x, clean, lg, sbuf, srecv, rg, tbuf, trecv, gl, gr, glrecv, grrecv,
           rcat, rwide, acc, inv_r,
           l_s, l_r, s_s, s_r, t_s, t_r, r_s, r_r, gl_s, gl_r, gr_s, gr_r, x_sem, o_sem):
    c = lax.axis_index("chan")
    t = lax.axis_index("tm")
    rank, lc = l0.shape
    rc = r0.shape[1]
    times = x.shape[1]
    width = 256

    def peer_t(s):
        return lax.rem(t + s, n)

    def peer_c(s):
        return lax.rem(c + s, m)

    def copy_t(src, dst, ssem, rsem, j):
        return pltpu.make_async_remote_copy(src_ref=src, dst_ref=dst, send_sem=ssem, recv_sem=rsem,
                                            device_id=(c, j), device_id_type=MESH)

    def copy_c(src, dst, ssem, rsem, j):
        return pltpu.make_async_remote_copy(src_ref=src, dst_ref=dst, send_sem=ssem, recv_sem=rsem,
                                            device_id=(j, t), device_id_type=MESH)

    def loop(first, last, body):
        def step(s, carry):
            body(s)
            return carry
        lax.fori_loop(first, last, step, 0)

    def left_copy(g, j, slot):
        src = l0 if g == 0 else lg.at[g, t]
        return copy_t(src, lg.at[g, slot], l_s.at[g, j], l_r.at[g, slot], j)

    def s_copy(i, j, slot):
        return copy_t(sbuf.at[i, j], srecv.at[i, slot], s_s.at[i, j], s_r.at[i, slot], j)

    def gr_copy(i, j, slot):
        return copy_t(gr.at[i], grrecv.at[i, slot], gr_s.at[i, j], gr_r.at[i, slot], j)

    def right_copy(g, j, slot):
        src = r0 if g == 0 else rg.at[g, c]
        return copy_c(src, rg.at[g, slot], r_s.at[g, j], r_r.at[g, slot], j)

    def t_copy(i, j, slot):
        return copy_c(tbuf.at[i, j], trecv.at[i, slot], t_s.at[i, j], t_r.at[i, slot], j)

    def gl_copy(i, j, slot):
        return copy_c(gl.at[i], glrecv.at[i, slot], gl_s.at[i, j], gl_r.at[i, slot], j)

    def rows_of(j):
        return pl.ds(pl.multiple_of(j * lc, lc), lc)

    def x_copy(j):
        return pltpu.make_async_copy(x_hbm.at[rows_of(j)], x.at[rows_of(j)], x_sem.at[j])

    def o_copy(j):
        return pltpu.make_async_copy(x.at[rows_of(j)], out_hbm.at[rows_of(j)], o_sem.at[j])

    loop(0, n, lambda s: x_copy(peer_t(s)).start())

    barrier = pltpu.get_barrier_semaphore()
    loop(1, n, lambda s: pl.semaphore_signal(barrier, inc=1, device_id=(c, peer_t(s)), device_id_type=MESH))
    loop(1, m, lambda s: pl.semaphore_signal(barrier, inc=1, device_id=(peer_c(s), t), device_id_type=MESH))
    pl.semaphore_wait(barrier, n + m - 2)

    loop(1, m, lambda s: right_copy(0, peer_c(s), c).start())
    loop(1, n, lambda s: left_copy(0, peer_t(s), t).start())
    lg[0, t] = l0[...]
    rg[0, c] = r0[...]

    rows = lax.broadcasted_iota(jnp.int32, (rank, rank), 0)
    cols = lax.broadcasted_iota(jnp.int32, (rank, rank), 1)
    ridge = jnp.where(rows == cols, RIDGE, 0.0).astype(jnp.float32)

    for i in range(ITERS):
        last = i == ITERS - 1

        loop(1, m, lambda s: right_copy(i, c, peer_c(s)).wait_recv())
        total = None
        for q in range(m):
            part = rg[i, q]
            both = stacked(part)
            high = both[:rank]
            low = both[rank:]
            at = pl.ds(q * rc, rc)
            rcat[:, at] = jnp.concatenate([high, high, low, low], axis=0).astype(jnp.bfloat16)
            rwide[at, :] = both.T.astype(jnp.bfloat16)
            term = outer_gram(part)
            total = term if total is None else total + term
        gr[i] = total
        grrecv[i, t] = total
        loop(1, n, lambda s: gr_copy(i, peer_t(s), t).start())

        def block_a(s):
            j = peer_t(s)

            @pl.when(s > 0)
            def _():
                left_copy(i, t, j).wait_recv() if i == 0 else None

            if i == 0:
                x_copy(j).wait()
            two = stacked(lg[i, j]).T.astype(jnp.bfloat16)
            lcat = jnp.concatenate([two, two], axis=1)
            at = rows_of(j)
            sums = jnp.zeros((lc, 2 * rank), jnp.float32)
            for b in range(times // width):
                part = pl.ds(b * width, width)
                values = x[at, part]
                residue = values - dot(lcat, rcat[:, part])
                outlier = residue - jnp.clip(residue, -LEVEL, LEVEL)
                high, low = split(values - outlier)
                if last:
                    x[at, part] = outlier
                clean[0, at, part] = high
                clean[1, at, part] = low
                sums += dot(high, rwide[part, :]) + dot(low, rwide[part, :])
            flat = sums.T
            sbuf[i, j] = flat[:rank] + flat[rank:]
            if last:
                o_copy(j).start()

            @pl.when(s > 0)
            def _():
                s_copy(i, j, t).start()

        loop(0, n, block_a)

        loop(1, n, lambda s: gr_copy(i, t, peer_t(s)).wait_recv())
        total = ridge
        for q in range(n):
            total = total + grrecv[i, q]
        inv_r[...] = inverse(total)

        def add_s(s, value):
            j = lax.rem(t + n - s, n)
            s_copy(i, t, j).wait_recv()
            return value + srecv[i, j]

        total = lax.fori_loop(1, n, add_s, sbuf[i, t])
        piece = jnp.dot(inv_r[...], total, precision=HIGHEST, preferred_element_type=jnp.float32)
        lg[i + 1, t] = piece
        loop(1, n, lambda s: left_copy(i + 1, peer_t(s), t).start())
        if last:
            lout[...] = piece

        acc[...] = jnp.zeros_like(acc)

        def block_b(s, gram):
            j = lax.rem(t + n - s, n)

            @pl.when(s > 0)
            def _():
                left_copy(i + 1, t, j).wait_recv()

            value = lg[i + 1, j]
            both = stacked(value).astype(jnp.bfloat16)
            at = rows_of(j)
            for b in range(times // width):
                part = pl.ds(b * width, width)
                acc[:, part] += dot(both, clean[0, at, part]) + dot(both, clean[1, at, part])
            return gram + outer_gram(value)

        gram = lax.fori_loop(0, n, block_b, jnp.zeros((rank, rank), jnp.float32))
        gl[i] = gram
        glrecv[i, c] = gram
        loop(1, m, lambda s: gl_copy(i, peer_c(s), c).start())
        for q in range(m):
            at = pl.ds(q * rc, rc)
            tbuf[i, q] = acc[:rank, at] + acc[rank:, at]
        loop(1, m, lambda s: t_copy(i, peer_c(s), c).start())
        loop(1, m, lambda s: gl_copy(i, c, peer_c(s)).wait_recv())
        total = ridge
        for q in range(m):
            total = total + glrecv[i, q]
        inv_l = inverse(total)

        def add_t(s, value):
            j = peer_c(s)
            t_copy(i, c, j).wait_recv()
            return value + trecv[i, j]

        total = lax.fori_loop(1, m, add_t, tbuf[i, c])
        piece = jnp.dot(inv_l, total, precision=HIGHEST, preferred_element_type=jnp.float32)
        if last:
            rout[...] = piece
        else:
            rg[i + 1, c] = piece
            loop(1, m, lambda s: right_copy(i + 1, peer_c(s), c).start())

    for i in range(ITERS):
        loop(1, n, lambda s: s_copy(i, peer_t(s), t).wait_send())
        loop(1, n, lambda s: gr_copy(i, peer_t(s), t).wait_send())
        loop(1, m, lambda s: t_copy(i, peer_c(s), c).wait_send())
        loop(1, m, lambda s: gl_copy(i, peer_c(s), c).wait_send())
        loop(1, m, lambda s: right_copy(i, peer_c(s), c).wait_send())
    for i in range(ITERS + 1):
        loop(1, n, lambda s: left_copy(i, peer_t(s), t).wait_send())
    loop(0, n, lambda s: o_copy(peer_t(s)).wait())


def shards(n, m, readings, channel_start, time_start):
    lc, rank = channel_start.shape
    rc = time_start.shape[0]
    rows, times = readings.shape
    f32 = jnp.float32
    vmem = pl.BlockSpec(memory_space=pltpu.VMEM)
    anywhere = pl.BlockSpec(memory_space=pl.ANY)
    dma = pltpu.SemaphoreType.DMA
    outliers, left, right = pl.pallas_call(
        functools.partial(kernel, n, m),
        out_shape=(jax.ShapeDtypeStruct((rows, times), f32),
                   jax.ShapeDtypeStruct((rank, lc), f32),
                   jax.ShapeDtypeStruct((rank, rc), f32)),
        in_specs=[anywhere, vmem, vmem],
        out_specs=(anywhere, vmem, vmem),
        scratch_shapes=[
            pltpu.VMEM((rows, times), f32),
            pltpu.VMEM((2, rows, times), jnp.bfloat16),
            pltpu.VMEM((ITERS + 1, n, rank, lc), f32),
            pltpu.VMEM((ITERS, n, rank, lc), f32),
            pltpu.VMEM((ITERS, n, rank, lc), f32),
            pltpu.VMEM((ITERS, m, rank, rc), f32),
            pltpu.VMEM((ITERS, m, rank, rc), f32),
            pltpu.VMEM((ITERS, m, rank, rc), f32),
            pltpu.VMEM((ITERS, rank, rank), f32),
            pltpu.VMEM((ITERS, rank, rank), f32),
            pltpu.VMEM((ITERS, m, rank, rank), f32),
            pltpu.VMEM((ITERS, n, rank, rank), f32),
            pltpu.VMEM((4 * rank, times), jnp.bfloat16),
            pltpu.VMEM((times, 2 * rank), jnp.bfloat16),
            pltpu.VMEM((2 * rank, times), f32),
            pltpu.VMEM((rank, rank), f32),
            dma((ITERS + 1, n)), dma((ITERS + 1, n)),
            dma((ITERS, n)), dma((ITERS, n)),
            dma((ITERS, m)), dma((ITERS, m)),
            dma((ITERS, m)), dma((ITERS, m)),
            dma((ITERS, m)), dma((ITERS, m)),
            dma((ITERS, n)), dma((ITERS, n)),
            dma((n,)), dma((n,)),
        ],
        compiler_params=pltpu.CompilerParams(collective_id=0, has_side_effects=True,
                                             vmem_limit_bytes=48 * 1024 * 1024),
    )(readings, channel_start.T, time_start.T)
    return outliers, left.T, right.T


def solution(mesh):
    n, m = mesh.shape["tm"], mesh.shape["chan"]
    specs = (P("chan", "tm"), P(("chan", "tm"), None), P(("tm", "chan"), None))
    return jax.shard_map(functools.partial(shards, n, m), mesh=mesh, in_specs=specs, out_specs=specs,
                         check_vma=False)
```

time: 454 us -> 121 us (0.27)
  the two profiles are of different devices: /device:TPU:0 before, /device:TPU:25 now
where the time goes in v1:
time: 121 us
  Pallas kernels  109 us (90%)
  local copies, waits for them, and re-layouts  11.4 us (9%)
    pallas_call x1, Pallas kernels, shards(): pl.pallas_call(functools.partial(kernel, n, m), out_shape=(jax.ShapeDtype...  109 us
    unnamed x7, local copies, waits for them, and re-layouts  11.4 us

profile of v1, /device:TPU:25, one launch (start us, length us, event | category | flops | bytes accessed | tf_op | source)
XLA Modules:
  0.0 121.3 jit_solution(18131709272874250716)
XLA Ops:
  0.6 0.0 copy-start
  0.6 0.8 copy-done
  1.5 0.0 copy-start.1
  1.5 0.8 copy-done.1
  2.3 109.2 %shard_map.58 = (f32[2048,1024]{1,0:T(8,128)}, f32[64,256]{1,0:T(8,128)S(1)}, f32[64,256]{1,0:T(8,128)S(1)}) custom-call(f32[2048,1024]{1,0:T(8,128)} %x_hbm.1, f32[64,256]{1,0:T(8,128)S(1)} %bitcast.4, f32[64,256]{1,0:T(8,128)S(1)} %bitcast.5), custom_call_target="tpu_custom_call" | custom-call | tf_op jit(solution)/shard_map/pallas_call | solution.py:262
  111.5 8.4 %copy.9 = f32[2048,1024]{1,0:T(8,128)} copy(f32[2048,1024]{1,0:T(8,128)} %get-tuple-element.12) | data formatting | bytes 16777216
  120.0 0.6 copy.10
  120.6 0.6 copy.11
Async XLA Ops:
  0.6 0.8 copy-start
  1.5 0.8 copy-start.1

commit v2 on v1

--- a/solution.py
+++ b/solution.py
@@ -38,26 +38,49 @@
     rank = gram.shape[0]
     rows = lax.broadcasted_iota(jnp.int32, (rank, rank), 0)
     cols = lax.broadcasted_iota(jnp.int32, (rank, rank), 1)
-    for k in range(rank):
-        row = gram[k:k + 1, :]
-        col = gram[:, k:k + 1]
-        inv = 1.0 / gram[k:k + 1, k:k + 1]
-        scaled = jnp.where(cols[:1] == k, 1.0, row) * inv
-        rest = jnp.where(cols == k, 0.0, gram) - col * scaled
-        gram = jnp.where(rows == k, scaled, rest)
+    lane = cols[:1]
+    for k in range(0, rank, 2):
+        up, down = gram[k:k + 1, :], gram[k + 1:k + 2, :]
+        first, second = gram[:, k:k + 1], gram[:, k + 1:k + 2]
+        wide = lambda value: jnp.broadcast_to(value, (1, rank))
+        p, q = wide(up[:, k:k + 1]), wide(up[:, k + 1:k + 2])
+        r, d = wide(down[:, k:k + 1]), wide(down[:, k + 1:k + 2])
+        inv = 1.0 / (p * d - q * r)
+        up = jnp.where(lane == k, 1.0, jnp.where(lane == k + 1, 0.0, up))
+        down = jnp.where(lane == k, 0.0, jnp.where(lane == k + 1, 1.0, down))
+        new_up = (d * up - q * down) * inv
+        new_down = (p * down - r * up) * inv
+        rest = jnp.where((cols == k) | (cols == k + 1), 0.0, gram) - first * new_up - second * new_down
+        gram = jnp.where(rows == k, new_up, jnp.where(rows == k + 1, new_down, rest))
     return gram
 
 
-def kernel(n, m, x_hbm, l0, r0, out_hbm, lout, rout,
-           x, clean, lg, sbuf, srecv, rg, tbuf, trecv, gl, gr, glrecv, grrecv,
+def kernel(n, m, x_hbm, l0, r0, x, lout, rout,
+           clean, lg, sbuf, precv, srecv, rg, tbuf, trecv, gl, gr, glrecv, grrecv,
            rcat, rwide, acc, inv_r,
-           l_s, l_r, s_s, s_r, t_s, t_r, r_s, r_r, gl_s, gl_r, gr_s, gr_r, x_sem, o_sem):
+           lz_s, lx_s, l_r, p_s, p_r, s_s, s_r, t_s, t_r, r_s, r_r, gl_s, gl_r, gr_s, gr_r, x_sem):
     c = lax.axis_index("chan")
     t = lax.axis_index("tm")
     rank, lc = l0.shape
     rc = r0.shape[1]
     times = x.shape[1]
     width = 256
+    half = n // 2
+    z, pair = t // 2, t % 2
+    other = z * 2 + 1 - pair
+
+    def flip(s):
+        value, bit = 0, 1
+        while bit < half:
+            value = value + bit * ((z // bit + s // bit) % 2)
+            bit *= 2
+        return value
+
+    def mine(q):
+        return q * 2 + pair
+
+    def theirs(q):
+        return q * 2 + 1 - pair
 
     def peer_t(s):
         return lax.rem(t + s, n)
@@ -79,12 +102,31 @@
             return carry
         lax.fori_loop(first, last, step, 0)
 
-    def left_copy(g, j, slot):
-        src = l0 if g == 0 else lg.at[g, t]
-        return copy_t(src, lg.at[g, slot], l_s.at[g, j], l_r.at[g, slot], j)
-
-    def s_copy(i, j, slot):
-        return copy_t(sbuf.at[i, j], srecv.at[i, slot], s_s.at[i, j], s_r.at[i, slot], j)
+    def left_src(g, q, own):
+        return l0 if own and g == 0 else lg.at[g, mine(q)]
+
+    def left_z(g, q, slot, own=True):
+        return copy_t(left_src(g, z, own), lg.at[g, slot], lz_s.at[g, q], l_r.at[g, slot], mine(q))
+
+    def left_x(g, q, slot, own):
+        return copy_t(left_src(g, q, own), lg.at[g, slot], lx_s.at[g, q], l_r.at[g, slot], other)
+
+    def left_send(g):
+        loop(1, half, lambda s: left_z(g, flip(s), t).start())
+        left_x(g, z, t, True).start()
+
+    def left_wait(g, q):
+        left_z(g, q, mine(q)).wait_recv()
+        left_x(g, q, mine(q), False).start()
+
+    def left_wait_other(g, q):
+        left_x(g, q, theirs(q), False).wait_recv()
+
+    def pair_copy(i, q, slot):
+        return copy_t(sbuf.at[i, theirs(q)], precv.at[i, slot], p_s.at[i, q], p_r.at[i, slot], other)
+
+    def s_copy(i, q, slot):
+        return copy_t(sbuf.at[i, mine(q)], srecv.at[i, slot], s_s.at[i, q], s_r.at[i, slot], mine(q))
 
     def gr_copy(i, j, slot):
         return copy_t(gr.at[i], grrecv.at[i, slot], gr_s.at[i, j], gr_r.at[i, slot], j)
@@ -105,10 +147,16 @@
     def x_copy(j):
         return pltpu.make_async_copy(x_hbm.at[rows_of(j)], x.at[rows_of(j)], x_sem.at[j])
 
-    def o_copy(j):
-        return pltpu.make_async_copy(x.at[rows_of(j)], out_hbm.at[rows_of(j)], o_sem.at[j])
-
-    loop(0, n, lambda s: x_copy(peer_t(s)).start())
+    def first_of(i, s):
+        q = flip(s)
+
+        @pl.when(s > 0)
+        def _():
+            left_wait(i, q)
+        return q
+
+    loop(0, half, lambda s: x_copy(mine(flip(s))).start())
+    loop(0, half, lambda s: x_copy(theirs(flip(s))).start())
 
     barrier = pltpu.get_barrier_semaphore()
     loop(1, n, lambda s: pl.semaphore_signal(barrier, inc=1, device_id=(c, peer_t(s)), device_id_type=MESH))
@@ -116,7 +164,7 @@
     pl.semaphore_wait(barrier, n + m - 2)
 
     loop(1, m, lambda s: right_copy(0, peer_c(s), c).start())
-    loop(1, n, lambda s: left_copy(0, peer_t(s), t).start())
+    left_send(0)
     lg[0, t] = l0[...]
     rg[0, c] = r0[...]
 
@@ -143,13 +191,7 @@
         grrecv[i, t] = total
         loop(1, n, lambda s: gr_copy(i, peer_t(s), t).start())
 
-        def block_a(s):
-            j = peer_t(s)
-
-            @pl.when(s > 0)
-            def _():
-                left_copy(i, t, j).wait_recv() if i == 0 else None
-
+        def block_a(j):
             if i == 0:
                 x_copy(j).wait()
             two = stacked(lg[i, j]).T.astype(jnp.bfloat16)
@@ -169,14 +211,37 @@
                 sums += dot(high, rwide[part, :]) + dot(low, rwide[part, :])
             flat = sums.T
             sbuf[i, j] = flat[:rank] + flat[rank:]
-            if last:
-                o_copy(j).start()
+
+        def own_a(s):
+            block_a(mine(first_of(0, s) if i == 0 else flip(s)))
+
+        def other_a(s):
+            q = flip(s)
+            if i == 0:
+                left_wait_other(0, q)
+            block_a(theirs(q))
+            pair_copy(i, q, q).start()
+
+        def join(s):
+            q = flip(s)
+            pair_copy(i, q, q).wait_recv()
+            sbuf[i, mine(q)] += precv[i, q]
 
             @pl.when(s > 0)
             def _():
-                s_copy(i, j, t).start()
-
-        loop(0, n, block_a)
+                s_copy(i, q, z).start()
+
+        def own_join(s):
+            own_a(half - 1 - s)
+            join(half - 1 - s)
+
+        if i == 0:
+            loop(0, half, own_a)
+            loop(0, half, lambda s: other_a(half - 1 - s))
+            loop(0, half, lambda s: join(half - 1 - s))
+        else:
+            loop(0, half, lambda s: other_a(half - 1 - s))
+            loop(0, half, own_join)
 
         loop(1, n, lambda s: gr_copy(i, t, peer_t(s)).wait_recv())
         total = ridge
@@ -185,26 +250,20 @@
         inv_r[...] = inverse(total)
 
         def add_s(s, value):
-            j = lax.rem(t + n - s, n)
-            s_copy(i, t, j).wait_recv()
-            return value + srecv[i, j]
-
-        total = lax.fori_loop(1, n, add_s, sbuf[i, t])
+            q = flip(s)
+            s_copy(i, z, q).wait_recv()
+            return value + srecv[i, q]
+
+        total = lax.fori_loop(1, half, add_s, sbuf[i, t])
         piece = jnp.dot(inv_r[...], total, precision=HIGHEST, preferred_element_type=jnp.float32)
         lg[i + 1, t] = piece
-        loop(1, n, lambda s: left_copy(i + 1, peer_t(s), t).start())
+        left_send(i + 1)
         if last:
             lout[...] = piece
 
         acc[...] = jnp.zeros_like(acc)
 
-        def block_b(s, gram):
-            j = lax.rem(t + n - s, n)
-
-            @pl.when(s > 0)
-            def _():
-                left_copy(i + 1, t, j).wait_recv()
-
+        def block_b(j, gram):
             value = lg[i + 1, j]
             both = stacked(value).astype(jnp.bfloat16)
             at = rows_of(j)
@@ -213,7 +272,16 @@
                 acc[:, part] += dot(both, clean[0, at, part]) + dot(both, clean[1, at, part])
             return gram + outer_gram(value)
 
-        gram = lax.fori_loop(0, n, block_b, jnp.zeros((rank, rank), jnp.float32))
+        def own_b(s, gram):
+            return block_b(mine(first_of(i + 1, s)), gram)
+
+        def other_b(s, gram):
+            q = flip(s)
+            left_wait_other(i + 1, q)
+            return block_b(theirs(q), gram)
+
+        gram = lax.fori_loop(0, half, own_b, jnp.zeros((rank, rank), jnp.float32))
+        gram = lax.fori_loop(0, half, other_b, gram)
         gl[i] = gram
         glrecv[i, c] = gram
         loop(1, m, lambda s: gl_copy(i, peer_c(s), c).start())
@@ -241,14 +309,15 @@
             loop(1, m, lambda s: right_copy(i + 1, peer_c(s), c).start())
 
     for i in range(ITERS):
-        loop(1, n, lambda s: s_copy(i, peer_t(s), t).wait_send())
+        loop(0, half, lambda s: pair_copy(i, s, s).wait_send())
+        loop(1, half, lambda s: s_copy(i, flip(s), z).wait_send())
         loop(1, n, lambda s: gr_copy(i, peer_t(s), t).wait_send())
         loop(1, m, lambda s: t_copy(i, peer_c(s), c).wait_send())
         loop(1, m, lambda s: gl_copy(i, peer_c(s), c).wait_send())
         loop(1, m, lambda s: right_copy(i, peer_c(s), c).wait_send())
-    for i in range(ITERS + 1):
-        loop(1, n, lambda s: left_copy(i, peer_t(s), t).wait_send())
-    loop(0, n, lambda s: o_copy(peer_t(s)).wait())
+    for g in range(ITERS + 1):
+        loop(1, half, lambda s: left_z(g, flip(s), t).wait_send())
+        loop(0, half, lambda s: left_x(g, s, t, False).wait_send())
 
 
 def shards(n, m, readings, channel_start, time_start):
@@ -257,7 +326,7 @@
     rows, times = readings.shape
     f32 = jnp.float32
     vmem = pl.BlockSpec(memory_space=pltpu.VMEM)
-    anywhere = pl.BlockSpec(memory_space=pl.ANY)
+    anywhere = pl.BlockSpec(memory_space=pltpu.HBM)
     dma = pltpu.SemaphoreType.DMA
     outliers, left, right = pl.pallas_call(
         functools.partial(kernel, n, m),
@@ -265,13 +334,13 @@
                    jax.ShapeDtypeStruct((rank, lc), f32),
                    jax.ShapeDtypeStruct((rank, rc), f32)),
         in_specs=[anywhere, vmem, vmem],
-        out_specs=(anywhere, vmem, vmem),
+        out_specs=(vmem, vmem, vmem),
         scratch_shapes=[
-            pltpu.VMEM((rows, times), f32),
             pltpu.VMEM((2, rows, times), jnp.bfloat16),
             pltpu.VMEM((ITERS + 1, n, rank, lc), f32),
             pltpu.VMEM((ITERS, n, rank, lc), f32),
-            pltpu.VMEM((ITERS, n, rank, lc), f32),
+            pltpu.VMEM((ITERS, n // 2, rank, lc), f32),
+            pltpu.VMEM((ITERS, n // 2, rank, lc), f32),
             pltpu.VMEM((ITERS, m, rank, rc), f32),
             pltpu.VMEM((ITERS, m, rank, rc), f32),
             pltpu.VMEM((ITERS, m, rank, rc), f32),
@@ -283,16 +352,17 @@
             pltpu.VMEM((times, 2 * rank), jnp.bfloat16),
             pltpu.VMEM((2 * rank, times), f32),
             pltpu.VMEM((rank, rank), f32),
-            dma((ITERS + 1, n)), dma((ITERS + 1, n)),
-            dma((ITERS, n)), dma((ITERS, n)),
+            dma((ITERS + 1, n // 2)), dma((ITERS + 1, n // 2)), dma((ITERS + 1, n)),
+            dma((ITERS, n // 2)), dma((ITERS, n // 2)),
+            dma((ITERS, n // 2)), dma((ITERS, n // 2)),
             dma((ITERS, m)), dma((ITERS, m)),
             dma((ITERS, m)), dma((ITERS, m)),
             dma((ITERS, m)), dma((ITERS, m)),
             dma((ITERS, n)), dma((ITERS, n)),
-            dma((n,)), dma((n,)),
+            dma((n,)),
         ],
         compiler_params=pltpu.CompilerParams(collective_id=0, has_side_effects=True,
-                                             vmem_limit_bytes=48 * 1024 * 1024),
+                                             vmem_limit_bytes=32 * 1024 * 1024),
     )(readings, channel_start.T, time_start.T)
     return outliers, left.T, right.T
 

time: 121 us -> 98.9 us (0.82)
  the two profiles are of different devices: /device:TPU:25 before, /device:TPU:0 now
where the time goes in v2:
time: 98.9 us; the launch traced here: 98.6 us
  Pallas kernels  88.3 us (89%)
  local copies, waits for them, and re-layouts  9.71 us (10%)
    pallas_call x1, Pallas kernels, shards(): pl.pallas_call(functools.partial(kernel, n, m), out_shape=(jax.ShapeDtype...  88.3 us
    unnamed x9, local copies, waits for them, and re-layouts  9.71 us

profile of v2, /device:TPU:0, one launch (start us, length us, event | category | flops | bytes accessed | tf_op | source)
XLA Modules:
  0.0 98.6 jit_solution(14779487262930892080)
XLA Ops:
  0.6 0.0 copy-start
  0.6 3.4 %copy-done = f32[2048,1024]{1,0:T(8,128)S(1)} copy-done((f32[2048,1024]{1,0:T(8,128)S(1)}, f32[2048,1024]{1,0:T(8,128)}, u32[]{:S(2)}) %copy-start) | copy-done | bytes 8388632
  4.0 0.0 copy-start.1
  4.0 0.8 copy-done.1
  4.9 0.0 copy-start.2
  4.9 0.8 copy-done.2
  5.7 88.3 %shard_map.58 = (f32[2048,1024]{1,0:T(8,128)S(1)}, f32[64,256]{1,0:T(8,128)S(1)}, f32[64,256]{1,0:T(8,128)S(1)}) custom-call(f32[2048,1024]{1,0:T(8,128)S(1)} %copy-done, f32[64,256]{1,0:T(8,128)S(1)} %bitcast.4, f32[64,256]{1,0:T(8,128)S(1)} %bitcast.5), custom_call_target="tpu_custom_call" | custom-call | tf_op jit(solution)/shard_map/pallas_call | solution.py:331
  94.0 3.4 %copy.9 = f32[2048,1024]{1,0:T(8,128)} copy(f32[2048,1024]{1,0:T(8,128)S(1)} %get-tuple-element.12) | data formatting | bytes 16777216
  97.4 0.6 copy.10
  98.0 0.6 copy.11
Async XLA Ops:
  0.6 3.4 %copy-start = (f32[2048,1024]{1,0:T(8,128)S(1)}, f32[2048,1024]{1,0:T(8,128)}, u32[]{:S(2)}) copy-start(f32[2048,1024]{1,0:T(8,128)} %x_hbm.1) | copy-start | bytes 25165828
  4.0 0.8 copy-start.1
  4.9 0.8 copy-start.2

commit v3 on v2

--- a/solution.py
+++ b/solution.py
@@ -32,6 +32,16 @@
 def outer_gram(value):
     return lax.dot_general(value, value, (((1,), (1,)), ((), ())), precision=HIGHEST,
                            preferred_element_type=jnp.float32)
+
+
+def packed(gram):
+    half = gram.shape[0] // 2
+    return jnp.concatenate([gram[:half], gram[half:]], axis=1)
+
+
+def unpacked(value):
+    rank = value.shape[0] * 2
+    return jnp.concatenate([value[:, :rank], value[:, rank:]], axis=0)
 
 
 def inverse(gram):
@@ -64,7 +74,7 @@
     rank, lc = l0.shape
     rc = r0.shape[1]
     times = x.shape[1]
-    width = 256
+    width = times
     half = n // 2
     z, pair = t // 2, t % 2
     other = z * 2 + 1 - pair
@@ -187,6 +197,7 @@
             rwide[at, :] = both.T.astype(jnp.bfloat16)
             term = outer_gram(part)
             total = term if total is None else total + term
+        total = packed(total)
         gr[i] = total
         grrecv[i, t] = total
         loop(1, n, lambda s: gr_copy(i, peer_t(s), t).start())
@@ -244,10 +255,10 @@
             loop(0, half, own_join)
 
         loop(1, n, lambda s: gr_copy(i, t, peer_t(s)).wait_recv())
-        total = ridge
-        for q in range(n):
+        total = grrecv[i, 0]
+        for q in range(1, n):
             total = total + grrecv[i, q]
-        inv_r[...] = inverse(total)
+        inv_r[...] = inverse(unpacked(total) + ridge)
 
         def add_s(s, value):
             q = flip(s)
@@ -282,6 +293,7 @@
 
         gram = lax.fori_loop(0, half, own_b, jnp.zeros((rank, rank), jnp.float32))
         gram = lax.fori_loop(0, half, other_b, gram)
+        gram = packed(gram)
         gl[i] = gram
         glrecv[i, c] = gram
         loop(1, m, lambda s: gl_copy(i, peer_c(s), c).start())
@@ -290,10 +302,10 @@
             tbuf[i, q] = acc[:rank, at] + acc[rank:, at]
         loop(1, m, lambda s: t_copy(i, peer_c(s), c).start())
         loop(1, m, lambda s: gl_copy(i, c, peer_c(s)).wait_recv())
-        total = ridge
-        for q in range(m):
+        total = glrecv[i, 0]
+        for q in range(1, m):
             total = total + glrecv[i, q]
-        inv_l = inverse(total)
+        inv_l = inverse(unpacked(total) + ridge)
 
         def add_t(s, value):
             j = peer_c(s)
@@ -344,10 +356,10 @@
             pltpu.VMEM((ITERS, m, rank, rc), f32),
             pltpu.VMEM((ITERS, m, rank, rc), f32),
             pltpu.VMEM((ITERS, m, rank, rc), f32),
-            pltpu.VMEM((ITERS, rank, rank), f32),
-            pltpu.VMEM((ITERS, rank, rank), f32),
-            pltpu.VMEM((ITERS, m, rank, rank), f32),
-            pltpu.VMEM((ITERS, n, rank, rank), f32),
+            pltpu.VMEM((ITERS, rank // 2, 2 * rank), f32),
+            pltpu.VMEM((ITERS, rank // 2, 2 * rank), f32),
+            pltpu.VMEM((ITERS, m, rank // 2, 2 * rank), f32),
+            pltpu.VMEM((ITERS, n, rank // 2, 2 * rank), f32),
             pltpu.VMEM((4 * rank, times), jnp.bfloat16),
             pltpu.VMEM((times, 2 * rank), jnp.bfloat16),
             pltpu.VMEM((2 * rank, times), f32),
@@ -362,7 +374,7 @@
             dma((n,)),
         ],
         compiler_params=pltpu.CompilerParams(collective_id=0, has_side_effects=True,
-                                             vmem_limit_bytes=32 * 1024 * 1024),
+                                             vmem_limit_bytes=42 * 1024 * 1024),
     )(readings, channel_start.T, time_start.T)
     return outliers, left.T, right.T
 

time: 98.9 us -> 91.6 us (0.926)
  Pallas kernels: 88.3 us -> 84.5 us
  local copies, waits for them, and re-layouts: 9.71 us -> 6.33 us
    pallas_call x1, Pallas kernels: 88.3 us -> 84.5 us  [shards(): pl.pallas_call(functools.partial(kernel, n, m), out_shape=(jax.ShapeDtype...]
    unnamed x9 -> x7, local copies, waits for them, and re-layouts: 9.71 us -> 6.33 us
where the time goes in v3:
time: 91.6 us; the launch traced here: 91.4 us
  Pallas kernels  84.5 us (92%)
  local copies, waits for them, and re-layouts  6.33 us (7%)
    pallas_call x1, Pallas kernels, shards(): pl.pallas_call(functools.partial(kernel, n, m), out_shape=(jax.ShapeDtype...  84.5 us
    unnamed x7, local copies, waits for them, and re-layouts  6.33 us

profile of v3, /device:TPU:0, one launch (start us, length us, event | category | flops | bytes accessed | tf_op | source)
XLA Modules:
  0.0 91.4 jit_solution(13220444322952551210)
XLA Ops:
  0.6 0.0 copy-start
  0.6 0.8 copy-done
  1.5 0.0 copy-start.1
  1.5 0.8 copy-done.1
  2.3 84.5 %shard_map.58 = (f32[2048,1024]{1,0:T(8,128)S(1)}, f32[64,256]{1,0:T(8,128)S(1)}, f32[64,256]{1,0:T(8,128)S(1)}) custom-call(f32[2048,1024]{1,0:T(8,128)} %x_hbm.1, f32[64,256]{1,0:T(8,128)S(1)} %bitcast.4, f32[64,256]{1,0:T(8,128)S(1)} %bitcast.5), custom_call_target="tpu_custom_call" | custom-call | tf_op jit(solution)/shard_map/pallas_call | solution.py:343
  86.8 3.4 %copy.9 = f32[2048,1024]{1,0:T(8,128)} copy(f32[2048,1024]{1,0:T(8,128)S(1)} %get-tuple-element.12) | data formatting | bytes 16777216
  90.2 0.6 copy.10
  90.8 0.6 copy.11
Async XLA Ops:
  0.6 0.8 copy-start
  1.5 0.8 copy-start.1

commit v4 on v3

--- a/solution.py
+++ b/solution.py
@@ -29,13 +29,14 @@
     return jnp.dot(first, second, preferred_element_type=jnp.float32)
 
 
-def outer_gram(value):
-    return lax.dot_general(value, value, (((1,), (1,)), ((), ())), precision=HIGHEST,
-                           preferred_element_type=jnp.float32)
-
-
-def packed(gram):
-    half = gram.shape[0] // 2
+def outer_gram(both):
+    return lax.dot_general(both, both, (((1,), (1,)), ((), ())), preferred_element_type=jnp.float32)
+
+
+def packed(parts):
+    rank = parts.shape[0] // 2
+    half = rank // 2
+    gram = (parts[:rank, :rank] + parts[rank:, rank:]) + (parts[:rank, rank:] + parts[rank:, :rank])
     return jnp.concatenate([gram[:half], gram[half:]], axis=1)
 
 
@@ -195,7 +196,7 @@
             at = pl.ds(q * rc, rc)
             rcat[:, at] = jnp.concatenate([high, high, low, low], axis=0).astype(jnp.bfloat16)
             rwide[at, :] = both.T.astype(jnp.bfloat16)
-            term = outer_gram(part)
+            term = outer_gram(both.astype(jnp.bfloat16))
             total = term if total is None else total + term
         total = packed(total)
         gr[i] = total
@@ -212,11 +213,12 @@
             for b in range(times // width):
                 part = pl.ds(b * width, width)
                 values = x[at, part]
-                residue = values - dot(lcat, rcat[:, part])
-                outlier = residue - jnp.clip(residue, -LEVEL, LEVEL)
-                high, low = split(values - outlier)
+                fitted = dot(lcat, rcat[:, part])
+                residue = values - fitted
+                clipped = jnp.clip(residue, -LEVEL, LEVEL)
+                high, low = split(fitted + clipped)
                 if last:
-                    x[at, part] = outlier
+                    x[at, part] = residue - clipped
                 clean[0, at, part] = high
                 clean[1, at, part] = low
                 sums += dot(high, rwide[part, :]) + dot(low, rwide[part, :])
@@ -281,7 +283,7 @@
             for b in range(times // width):
                 part = pl.ds(b * width, width)
                 acc[:, part] += dot(both, clean[0, at, part]) + dot(both, clean[1, at, part])
-            return gram + outer_gram(value)
+            return gram + outer_gram(both)
 
         def own_b(s, gram):
             return block_b(mine(first_of(i + 1, s)), gram)
@@ -291,7 +293,7 @@
             left_wait_other(i + 1, q)
             return block_b(theirs(q), gram)
 
-        gram = lax.fori_loop(0, half, own_b, jnp.zeros((rank, rank), jnp.float32))
+        gram = lax.fori_loop(0, half, own_b, jnp.zeros((2 * rank, 2 * rank), jnp.float32))
         gram = lax.fori_loop(0, half, other_b, gram)
         gram = packed(gram)
         gl[i] = gram

time: 91.6 us -> 91.9 us (level)
  no operation moved by 1% of the time
where the time goes in v4:
time: 91.9 us; the launch traced here: 91.7 us
  Pallas kernels  84.7 us (92%)
  local copies, waits for them, and re-layouts  6.33 us (7%)
    pallas_call x1, Pallas kernels, shards(): pl.pallas_call(functools.partial(kernel, n, m), out_shape=(jax.ShapeDtype...  84.7 us
    unnamed x7, local copies, waits for them, and re-layouts  6.33 us

profile of v4, /device:TPU:0, one launch (start us, length us, event | category | flops | bytes accessed | tf_op | source)
XLA Modules:
  0.0 91.7 jit_solution(12296447705877306255)
XLA Ops:
  0.6 0.0 copy-start
  0.6 0.8 copy-done
  1.5 0.0 copy-start.1
  1.5 0.8 copy-done.1
  2.3 84.7 %shard_map.58 = (f32[2048,1024]{1,0:T(8,128)S(1)}, f32[64,256]{1,0:T(8,128)S(1)}, f32[64,256]{1,0:T(8,128)S(1)}) custom-call(f32[2048,1024]{1,0:T(8,128)} %x_hbm.1, f32[64,256]{1,0:T(8,128)S(1)} %bitcast.4, f32[64,256]{1,0:T(8,128)S(1)} %bitcast.5), custom_call_target="tpu_custom_call" | custom-call | tf_op jit(solution)/shard_map/pallas_call | solution.py:345
  87.0 3.4 %copy.9 = f32[2048,1024]{1,0:T(8,128)} copy(f32[2048,1024]{1,0:T(8,128)S(1)} %get-tuple-element.12) | data formatting | bytes 16777216
  90.4 0.6 copy.10
  91.1 0.6 copy.11
Async XLA Ops:
  0.6 0.8 copy-start
  1.5 0.8 copy-start.1
